TPU v7x, 32 devices: a whole 2x2x4 slice. The times are simulated.
32 devices in a mesh: dp: 8 (over y, x, core), tensor: 4 (over z).
Axes of the slice: x: 2, y: 2, z: 4, core: 2. Of those that a mesh axis runs over, the one named last changes fastest.
Arguments:
- tokens: bfloat16 [8192, 1536], P('dp'), may hold values from -6 to 6
- block_order: int32 [1, 8], replicated, may hold values from 0 to 7, each once within a row
- attn_gain: float32 [1536], replicated, may hold values from 0.5 to 1.5
- w_query: bfloat16 [1536, 1536], P(None, 'tensor'), may hold values from -0.15625 to 0.15625
- w_key: bfloat16 [1536, 768], P(None, 'tensor'), may hold values from -0.15625 to 0.15625
- w_value: bfloat16 [1536, 768], P(None, 'tensor'), may hold values from -0.15625 to 0.15625
- w_out: bfloat16 [1536, 1536], P('tensor'), may hold values from -1.25 to 1.25
- mlp_gain: float32 [1536], replicated, may hold values from 0.5 to 1.5
- w_gate: bfloat16 [1536, 4096], P(None, 'tensor'), may hold values from -0.15625 to 0.15625
- w_up: bfloat16 [1536, 4096], P(None, 'tensor'), may hold values from -0.15625 to 0.15625
- w_down: bfloat16 [4096, 1536], P('tensor'), may hold values from -0.09375 to 0.09375
- cotangent: bfloat16 [8192, 1536], P('dp'), may hold values from -6 to 6
Outputs:
- activations: bfloat16 [8192, 1536], P('dp')
- grad_tokens: bfloat16 [8192, 1536], P('dp')
- grad_attn_gain: float32 [1536], replicated
- grad_query: float32 [1536, 1536], P(None, 'tensor')
- grad_key: float32 [1536, 768], P(None, 'tensor')
- grad_value: float32 [1536, 768], P(None, 'tensor')
- grad_out: float32 [1536, 1536], P('tensor')
- grad_mlp_gain: float32 [1536], replicated
- grad_gate: float32 [1536, 4096], P(None, 'tensor')
- grad_up: float32 [1536, 4096], P(None, 'tensor')
- grad_down: float32 [4096, 1536], P('tensor')
Inputs may be any that keep to these rules, and one draw needn't show every extreme that they name: `block_order`: entry j of row g is the prompt block of 512 tokens held by the j-th device of group g; each row is a permutation.
All inputs are finite; a program needn't handle non-finite values.
Results may differ from a plain program's by a relative error of at most 0.02.
Values may be sent and summed in bfloat16 or wider, within the bound.
A program may use at most 192 MiB of HBM per device.

v0:
```python
import jax
import jax.numpy as jnp
from jax import lax
from jax.sharding import PartitionSpec as P

HEAD_DIM = 96
GROUP_DEVS = 8
PB = 512
CL = 512
EPSILON = 1e-05
ROTARY_BASE = 100000.0


def from_partner(value, axis, distance):
    mask = 2**distance
    pairs = [(source, source ^ mask) for source in range(lax.axis_size(axis))]
    return lax.ppermute(value, axis, pairs)


def rotary_tables(places):
    halfway = HEAD_DIM // 2
    frequency = ROTARY_BASE ** (-(jnp.arange(halfway, dtype=jnp.float32) * 2.0) / HEAD_DIM)
    angle = places.astype(jnp.float32)[:, None] * frequency[None, :]
    cosine_table = jnp.concatenate([jnp.cos(angle), jnp.cos(angle)], axis=-1)
    sine_table = jnp.concatenate([jnp.sin(angle), jnp.sin(angle)], axis=-1)
    return (cosine_table, sine_table)


def rotate(inputs, cosine_table, sine_table):
    halfway = inputs.shape[-1] // 2
    shaped = (inputs.shape[0],) + (1,) * (inputs.ndim - 2) + (inputs.shape[-1],)
    turned = jnp.concatenate([-inputs[..., halfway:], inputs[..., :halfway]], axis=-1)
    return inputs * cosine_table.reshape(shaped) + turned * sine_table.reshape(shaped)


def product(former, latter):
    return jnp.dot(former, latter, preferred_element_type=jnp.float32)


def weight_grad(former, latter):
    return lax.dot_general(
        former, latter, (((0,), (0,)), ((), ())), preferred_element_type=jnp.float32
    )


def input_grad(former, latter):
    return lax.dot_general(
        former, latter, (((1,), (1,)), ((), ())), preferred_element_type=jnp.float32
    )


def rms_inverse(inputs):
    return lax.rsqrt(jnp.mean(inputs * inputs, axis=-1, keepdims=True) + EPSILON)


def norm_back(inputs, inverse, gain, upstream):
    inner = upstream * gain
    through = inverse * inner - inputs * inverse**3 * jnp.mean(
        inner * inputs, axis=-1, keepdims=True
    )
    return (through, jnp.sum(upstream * inputs * inverse, axis=0))


def shards(
    tokens,
    block_order,
    attn_gain,
    w_query,
    w_key,
    w_value,
    w_out,
    mlp_gain,
    w_gate,
    w_up,
    w_down,
    cotangent,
):
    device = lax.axis_index("dp")
    member = device % GROUP_DEVS
    group_index = device // GROUP_DEVS
    order_row = lax.dynamic_index_in_dim(block_order, group_index, 0, keepdims=False)
    own_block = lax.dynamic_index_in_dim(order_row, member, 0, keepdims=False)
    offsets = jnp.arange(PB, dtype=jnp.int32)
    prompt_places = order_row[:, None] * PB + offsets[None, :]
    tail_places = GROUP_DEVS * PB + jnp.arange(CL, dtype=jnp.int32)
    places = jnp.concatenate([own_block * PB + offsets, tail_places])
    cosine_table, sine_table = rotary_tables(places)
    token_count = tokens.shape[0]
    key_heads = w_key.shape[1] // HEAD_DIM
    repeat = w_query.shape[1] // HEAD_DIM // key_heads
    factor = HEAD_DIM ** (-0.5)
    inputs = tokens.astype(jnp.float32)
    inverse_one = rms_inverse(inputs)
    normed = (inputs * inverse_one * attn_gain).astype(jnp.bfloat16)
    queries = rotate(
        product(normed, w_query).reshape(token_count, key_heads, repeat, HEAD_DIM),
        cosine_table,
        sine_table,
    ).astype(jnp.bfloat16)
    key_set = rotate(
        product(normed, w_key).reshape(token_count, key_heads, HEAD_DIM), cosine_table, sine_table
    ).astype(jnp.bfloat16)
    value_set = (
        product(normed, w_value).reshape(token_count, key_heads, HEAD_DIM).astype(jnp.bfloat16)
    )
    levels = GROUP_DEVS.bit_length() - 1
    stacked = jnp.stack([key_set[:PB], value_set[:PB]])[:, None]
    for level in range(levels):
        partner = from_partner(stacked, "dp", level)
        upper = member // 2**level % 2 == 1
        stacked = jnp.where(
            upper,
            jnp.concatenate([partner, stacked], axis=1),
            jnp.concatenate([stacked, partner], axis=1),
        )
    prompt_keys = stacked[0]
    prompt_values = stacked[1]
    tail_keys = key_set[PB:]
    tail_values = value_set[PB:]

    def scores(key_block, key_places):
        products = (
            jnp.einsum("qkrd,nkd->krqn", queries, key_block, preferred_element_type=jnp.float32)
            * factor
        )
        visible = key_places[None, None, None, :] <= places[None, None, :, None]
        return (products, visible)

    def total_step(running, block):
        summit, totals = running
        products, visible = scores(block[0], block[1])
        masked = jnp.where(visible, products, -1e30)
        higher = jnp.maximum(summit, jnp.max(masked, axis=-1))
        totals = totals * jnp.exp(summit - higher) + jnp.sum(
            jnp.where(visible, jnp.exp(masked - higher[..., None]), 0.0), axis=-1
        )
        return ((higher, totals), None)

    start = (
        jnp.full((key_heads, repeat, token_count), -1e30, jnp.float32),
        jnp.zeros((key_heads, repeat, token_count), jnp.float32),
    )
    running, _ = lax.scan(total_step, start, (prompt_keys, prompt_places))
    running, _ = total_step(running, (tail_keys, tail_places))
    log_total = running[0] + jnp.log(running[1])

    def chances_of(products, visible):
        return jnp.where(visible, jnp.exp(products - log_total[..., None]), 0.0)

    def output_step(summed, block):
        products, visible = scores(block[0], block[2])
        weights = chances_of(products, visible).astype(jnp.bfloat16)
        return (
            summed
            + jnp.einsum("krqn,nkd->qkrd", weights, block[1], preferred_element_type=jnp.float32),
            None,
        )

    empty_heads = jnp.zeros((token_count, key_heads, repeat, HEAD_DIM), jnp.float32)
    attended, _ = lax.scan(output_step, empty_heads, (prompt_keys, prompt_values, prompt_places))
    attended, _ = output_step(attended, (tail_keys, tail_values, tail_places))
    attended_low = attended.reshape(token_count, -1).astype(jnp.bfloat16)
    attention = lax.psum(product(attended_low, w_out).astype(jnp.bfloat16), "tensor").astype(
        jnp.float32
    )
    middle = inputs + attention
    inverse_two = rms_inverse(middle)
    normed_two = (middle * inverse_two * mlp_gain).astype(jnp.bfloat16)
    gate_pre = product(normed_two, w_gate)
    up_pre = product(normed_two, w_up)
    sigmoid_gate = jax.nn.sigmoid(gate_pre)
    hidden = (gate_pre * sigmoid_gate * up_pre).astype(jnp.bfloat16)
    feed_out = lax.psum(product(hidden, w_down).astype(jnp.bfloat16), "tensor").astype(jnp.float32)
    activations = (middle + feed_out).astype(jnp.bfloat16)
    upstream = cotangent.astype(jnp.float32)
    grad_hidden = input_grad(cotangent, w_down)
    grad_gate_low = (
        grad_hidden * up_pre * sigmoid_gate * (1.0 + gate_pre * (1.0 - sigmoid_gate))
    ).astype(jnp.bfloat16)
    grad_up_low = (grad_hidden * gate_pre * sigmoid_gate).astype(jnp.bfloat16)
    grad_w_gate = weight_grad(normed_two, grad_gate_low)
    grad_w_up = weight_grad(normed_two, grad_up_low)
    grad_w_down = weight_grad(hidden, cotangent)
    grad_normed_two = lax.psum(
        (input_grad(grad_gate_low, w_gate) + input_grad(grad_up_low, w_up)).astype(jnp.bfloat16),
        "tensor",
    ).astype(jnp.float32)
    through_two, grad_gain_two = norm_back(middle, inverse_two, mlp_gain, grad_normed_two)
    grad_middle = upstream + through_two
    grad_attention = grad_middle.astype(jnp.bfloat16)
    grad_w_out = weight_grad(attended_low, grad_attention)
    grad_attended = (
        input_grad(grad_attention, w_out)
        .reshape(token_count, key_heads, repeat, HEAD_DIM)
        .astype(jnp.bfloat16)
    )
    row_inner = jnp.transpose(
        jnp.sum(grad_attended.astype(jnp.float32) * attended, axis=-1), (1, 2, 0)
    )

    def back_step(grad_queries, block):
        products, visible = scores(block[0], block[2])
        chances = chances_of(products, visible)
        grad_chances = jnp.einsum(
            "qkrd,nkd->krqn", grad_attended, block[1], preferred_element_type=jnp.float32
        )
        grad_scores = (chances * (grad_chances - row_inner[..., None])).astype(jnp.bfloat16)
        grad_queries = (
            grad_queries
            + jnp.einsum(
                "krqn,nkd->qkrd", grad_scores, block[0], preferred_element_type=jnp.float32
            )
            * factor
        )
        grad_keys = (
            jnp.einsum("krqn,qkrd->nkd", grad_scores, queries, preferred_element_type=jnp.float32)
            * factor
        )
        grad_values = jnp.einsum(
            "krqn,qkrd->nkd",
            chances.astype(jnp.bfloat16),
            grad_attended,
            preferred_element_type=jnp.float32,
        )
        return (grad_queries, (grad_keys, grad_values))

    grad_queries, prompt_grads = lax.scan(
        back_step, empty_heads, (prompt_keys, prompt_values, prompt_places)
    )
    grad_queries, tail_grads = back_step(grad_queries, (tail_keys, tail_values, tail_places))
    pending = jnp.stack([prompt_grads[0], prompt_grads[1]])
    for level in reversed(range(levels)):
        halfway = pending.shape[1] // 2
        upper = member // 2**level % 2 == 1
        kept_part = jnp.where(upper, pending[:, halfway:], pending[:, :halfway])
        sent_part = jnp.where(upper, pending[:, :halfway], pending[:, halfway:])
        pending = kept_part + from_partner(sent_part.astype(jnp.bfloat16), "dp", level).astype(
            sent_part.dtype
        )
    grad_key_rot = jnp.concatenate([pending[0, 0], tail_grads[0]])
    grad_value_all = jnp.concatenate([pending[1, 0], tail_grads[1]])
    grad_query_low = (
        rotate(grad_queries, cosine_table, -sine_table)
        .reshape(token_count, -1)
        .astype(jnp.bfloat16)
    )
    grad_key_low = (
        rotate(grad_key_rot, cosine_table, -sine_table)
        .reshape(token_count, -1)
        .astype(jnp.bfloat16)
    )
    grad_value_low = grad_value_all.reshape(token_count, -1).astype(jnp.bfloat16)
    grad_w_query = weight_grad(normed, grad_query_low)
    grad_w_key = weight_grad(normed, grad_key_low)
    grad_w_value = weight_grad(normed, grad_value_low)
    grad_normed = lax.psum(
        (
            input_grad(grad_query_low, w_query)
            + input_grad(grad_key_low, w_key)
            + input_grad(grad_value_low, w_value)
        ).astype(jnp.bfloat16),
        "tensor",
    ).astype(jnp.float32)
    through_one, grad_gain_one = norm_back(inputs, inverse_one, attn_gain, grad_normed)
    grad_tokens = (grad_middle + through_one).astype(jnp.bfloat16)
    shares = (
        lax.psum_scatter(grad_gain_one, "dp", scatter_dimension=0, tiled=True),
        lax.psum_scatter(grad_w_query, "dp", scatter_dimension=0, tiled=True),
        lax.psum_scatter(grad_w_key, "dp", scatter_dimension=0, tiled=True),
        lax.psum_scatter(grad_w_value, "dp", scatter_dimension=0, tiled=True),
        lax.psum_scatter(grad_w_out, "dp", scatter_dimension=1, tiled=True),
        lax.psum_scatter(grad_gain_two, "dp", scatter_dimension=0, tiled=True),
        lax.psum_scatter(grad_w_gate, "dp", scatter_dimension=0, tiled=True),
        lax.psum_scatter(grad_w_up, "dp", scatter_dimension=0, tiled=True),
        lax.psum_scatter(grad_w_down, "dp", scatter_dimension=1, tiled=True),
    )
    summed_grads = (
        lax.all_gather(shares[0].astype(jnp.bfloat16), "dp", axis=0, tiled=True).astype(
            jnp.float32
        ),
        lax.all_gather(shares[1].astype(jnp.bfloat16), "dp", axis=0, tiled=True).astype(
            jnp.float32
        ),
        lax.all_gather(shares[2].astype(jnp.bfloat16), "dp", axis=0, tiled=True).astype(
            jnp.float32
        ),
        lax.all_gather(shares[3].astype(jnp.bfloat16), "dp", axis=0, tiled=True).astype(
            jnp.float32
        ),
        lax.all_gather(shares[4].astype(jnp.bfloat16), "dp", axis=1, tiled=True).astype(
            jnp.float32
        ),
        lax.all_gather(shares[5].astype(jnp.bfloat16), "dp", axis=0, tiled=True).astype(
            jnp.float32
        ),
        lax.all_gather(shares[6].astype(jnp.bfloat16), "dp", axis=0, tiled=True).astype(
            jnp.float32
        ),
        lax.all_gather(shares[7].astype(jnp.bfloat16), "dp", axis=0, tiled=True).astype(
            jnp.float32
        ),
        lax.all_gather(shares[8].astype(jnp.bfloat16), "dp", axis=1, tiled=True).astype(
            jnp.float32
        ),
    )
    return (activations, grad_tokens) + tuple(summed_grads)


def solution(mesh):
    in_specs = (
        P("dp", None),
        P(),
        P(),
        P(None, "tensor"),
        P(None, "tensor"),
        P(None, "tensor"),
        P("tensor", None),
        P(),
        P(None, "tensor"),
        P(None, "tensor"),
        P("tensor", None),
        P("dp", None),
    )
    out_specs = (
        P("dp", None),
        P("dp", None),
        P(),
        P(None, "tensor"),
        P(None, "tensor"),
        P(None, "tensor"),
        P("tensor", None),
        P(),
        P(None, "tensor"),
        P(None, "tensor"),
        P("tensor", None),
    )
    return jax.shard_map(shards, mesh=mesh, in_specs=in_specs, out_specs=out_specs, check_vma=False)
```

profile of v0, /device:TPU:0, one launch (start us, length us, event | category | flops | bytes accessed | tf_op | source)
XLA Modules:
  0.0 1503.1 jit_solution(2448952385256326114)
XLA Ops:
  32.2 14.5 collective-permute-done.1
  62.4 6.5 fusion.59
  68.9 17.4 %collective-permute-done.2 = bf16[2,4,512,2,96]{2,4,3,0,1:T(8,128)(2,1)} collective-permute-done((bf16[2,4,512,2,96]{2,4,3,0,1:T(8,128)(2,1)}, bf16[2,4,512,2,96]{2,4,3,0,1:T(8,128)(2,1)}, u32[]{:S(2)}, u32[]{:S(2)}) %collective-permute-start.2) | collective-permute-done | bytes 1572896 | tf_op jit(solution)/shard_map/ppermute | solution.py:17
  91.4 92.3 %while.39 = (s32[]{:T(128)}, f32[2,2,1024]{2,1,0:T(2,128)S(1)}, f32[2,2,1024]{2,1,0:T(2,128)S(1)}, s32[8,512]{1,0:T(8,128)S(1)}, s32[1024]{0:T(1024)S(1)}, /*ind...) while((s32[]{:T(128)}, f32[2,2,1024]{2,1,0:T(2,128)S(1)}, ...), condition=%wide.region_4.5_spmd.clone, body=%wide.region_1.4_spmd.clone.sunk | while | flops 419975168 | bytes 21654152 | solution.py:143
  114.9 6.4 fusion.203
  189.0 74.2 %while.40 = (s32[]{:T(128)}, f32[1024,2,2,96]{0,3,2,1:T(8,128)}, bf16[8,512,2,96]{1,3,2,0:T(8,128)(2,1)}, s32[8,512]{1,0:T(8,128)S(1)}, s32[1024]{0:T(1024)S(1)}...) while((s32[]{:T(128)}, f32[1024,2,2,96]{0,3,2,1:T(8,128)}, ...), condition=%wide.region_8.9_spmd.clone, body=%wide.region_7.8_spmd.clone.sunk | while | flops 815005696 | bytes 6646447 | solution.py:160
  263.2 7.2 fusion.99
  274.8 122.4 %all-reduce.11.cloned.1.call-done = bf16[1024,1536]{1,0:T(8,128)(2,1)} async-done(((bf16[1024,1536]{1,0:T(8,128)(2,1)}), bf16[1024,1536]{1,0:T(8,128)(2,1)}) %all-reduce.11.cloned.1.call-update) | async-done | bytes 3145744 | tf_op jit(solution)/shard_map/psum | solution.py:163
  412.4 8.3 multiply_convert_fusion.1
  431.5 120.2 %all-reduce.13.cloned.1.call-done = bf16[1024,1536]{1,0:T(8,128)(2,1)} async-done(((bf16[1024,1536]{1,0:T(8,128)(2,1)}), bf16[1024,1536]{1,0:T(8,128)(2,1)}) %all-reduce.13.cloned.1.call-update) | async-done | bytes 3145744 | tf_op jit(solution)/shard_map/psum | solution.py:184
  551.7 7.0 fusion.71
  571.7 181.7 %while.41 = (s32[]{:T(128)}, f32[1024,2,2,96]{0,3,2,1:T(8,128)}, f32[8,512,2,96]{1,3,2,0:T(8,128)}, f32[8,512,2,96]{1,3,2,0:T(8,128)}, bf16[8,512,2,96]{1,3,2,0:...) while((s32[]{:T(128)}, f32[1024,2,2,96]{0,3,2,1:T(8,128)}, ...), condition=%wide.region_16.17_spmd.clone, body=%wide.region_15.16_spmd.clone.sunk | while | flops 2036039680 | bytes 111014752 | solution.py:227
  767.3 8.7 fusion.124
  776.1 9.0 fusion.125
  785.1 8.7 fusion.126
  799.0 37.8 %collective-permute-done.3 = bf16[2,4,512,2,96]{2,4,3,1,0:T(8,128)(2,1)S(1)} collective-permute-done((bf16[2,4,512,2,96]{2,4,3,1,0:T(8,128)(2,1)S(1)}, bf16[2,4,512,2,96]{2,4,3,1,0:T(8,128)(2,1)S(1)}, u32[]{:S(2)}, u32[]{:S(2)}) %collective-permute-start.3) | collective-permute-done | bytes 1572896 | tf_op jit(solution)/shard_map/ppermute | solution.py:17
  842.3 33.1 %collective-permute-done.4 = bf16[2,2,512,2,96]{2,4,3,1,0:T(8,128)(2,1)S(1)} collective-permute-done((bf16[2,2,512,2,96]{2,4,3,1,0:T(8,128)(2,1)S(1)}, bf16[2,2,512,2,96]{2,4,3,1,0:T(8,128)(2,1)S(1)}, u32[]{:S(2)}, u32[]{:S(2)}) %collective-permute-start.4) | collective-permute-done | bytes 786464 | tf_op jit(solution)/shard_map/ppermute | solution.py:17
  894.9 6.5 convolution_convert_fusion.1
  909.5 50.2 %reduce-scatter.18.cloned.1.call-done = f32[192,1024]{1,0:T(8,128)} async-done(((f32[1536,1024]{1,0:T(8,128)}), f32[192,1024]{1,0:T(8,128)}) %reduce-scatter.18.cloned.1.call-update) | async-done | bytes 786448 | tf_op jit(solution)/shard_map/reduce_scatter | solution.py:274
  961.7 63.1 %reduce-scatter.20.cloned.1.call-done = f32[1024,192]{0,1:T(8,128)} async-done(((f32[1024,1536]{0,1:T(8,128)}), f32[1024,192]{0,1:T(8,128)}) %reduce-scatter.20.cloned.1.call-update) | async-done | bytes 786448 | tf_op jit(solution)/shard_map/reduce_scatter | solution.py:275
  1028.7 38.3 %reduce-scatter.12.cloned.1.call-done = f32[192,192]{1,0:T(8,128)} async-done(((f32[1536,192]{1,0:T(8,128)}), f32[192,192]{1,0:T(8,128)}) %reduce-scatter.12.cloned.1.call-update) | async-done | bytes 147472 | tf_op jit(solution)/shard_map/reduce_scatter | solution.py:270
  1067.9 11.3 all_gather.30
  1081.7 27.5 %reduce-scatter.10.cloned.1.call-done = f32[192,192]{1,0:T(8,128)} async-done(((f32[1536,192]{1,0:T(8,128)}), f32[192,192]{1,0:T(8,128)}) %reduce-scatter.10.cloned.1.call-update) | async-done | bytes 147472 | tf_op jit(solution)/shard_map/reduce_scatter | solution.py:269
  1110.1 11.3 all_gather.29
  1123.8 11.3 all-gather.8.cloned.1.call-done
  1137.8 24.0 %all-gather.6.cloned.1.call-done = bf16[1536,384]{1,0:T(8,128)(2,1)} async-done(((bf16[192,384]{1,0:T(8,128)(2,1)}), bf16[1536,384]{1,0:T(8,128)(2,1)}) %all-gather.6.cloned.1.call-update) | async-done | bytes 1179664 | tf_op jit(solution)/shard_map/all_gather | solution.py:281
  1164.6 223.4 %all-reduce.15.cloned.1.call-done = (bf16[1024,1536]{1,0:T(8,128)(2,1)}, bf16[1024,1536]{1,0:T(8,128)(2,1)}) async-done(((bf16[1024,1536]{1,0:T(8,128)(2,1)}, bf16[1024,1536]{1,0:T(8,128)(2,1)}), (bf16[1024,1536]{1,0:T(8,128)(2,1)}, bf16[1024,1536]{1,0:T(8,128)(2,1)})) %all-reduce.15.cloned.1.call-update) | async-done | bytes 6291472 | tf_op jit(solution)/shard_map/psum | solution.py:173
  1392.5 24.4 %all-reduce.4 = (bf16[1536]{0:T(1024)(128)(2,1)S(1)}, bf16[1536]{0:T(1024)(128)(2,1)S(1)}) all-reduce(f32[1536]{0:T(1024)S(1)} %get-tuple-element.291, f32[1536]{0:T(1024)S(1)} %copy-done.62), channel_id=2, replica_groups=mesh['dp'=8,'tensor'=4] {'dp'}, use_global_device_ids=true, to_apply=%region_20.21.clone | all-reduce | flops 3072 | bytes 18432
  1417.5 12.4 all-reduce.5
  1431.1 10.3 fusion.66
  1446.8 9.6 all-gather.12.cloned.1.call-done
  1461.8 28.9 %all-gather.14.cloned.1.call-done = bf16[1024,1536]{0,1:T(8,128)(2,1)} async-done(((bf16[1024,192]{0,1:T(8,128)(2,1)}), bf16[1024,1536]{0,1:T(8,128)(2,1)}) %all-gather.14.cloned.1.call-update) | async-done | bytes 3145744 | tf_op jit(solution)/shard_map/all_gather | solution.py:302
  (582 shorter events, 524.8 us)
Async XLA Ops:
  7.2 405.2 %copy-start = (bf16[1024,1536]{1,0:T(8,128)(2,1)S(1)}, bf16[1024,1536]{1,0:T(8,128)(2,1)}, u32[]{:S(2)}) copy-start(bf16[1024,1536]{1,0:T(8,128)(2,1)} %param.28) | copy-start | bytes 9437188
  7.2 390.0 %all-reduce.11.cloned.1.call-start = ((), (), s32[]{:S(2)}) async-start(), calls=%async_computation.7 | async-start | bytes 6291456 | tf_op jit(solution)/shard_map/psum | solution.py:163
  11.7 41.5 %copy-start.16 = (f32[1024,96]{0,1:T(8,128)}, f32[1024,96]{0,1:T(8,128)S(1)}, u32[]{:S(2)}) copy-start(f32[1024,96]{0,1:T(8,128)S(1)} %pad_maximum_fusion.2) | copy-start | bytes 1179652
  21.1 2.1 collective-permute-start
  25.7 21.0 %collective-permute-start.1 = (bf16[2,2,512,2,96]{2,4,3,0,1:T(8,128)(2,1)}, bf16[2,2,512,2,96]{2,4,3,0,1:T(8,128)(2,1)}, u32[]{:S(2)}, u32[]{:S(2)}) collective-permute-start(bf16[2,2,512,2,96]{2,4,3,0,1:T(8,128)(2,1)} %maximum_select_fusion.2), channel_id=1, source_target_pairs={{0,8},{4,12},{8,0},{12,4},{16,24},{20,28},{24,16},{28,20},{1,9},{5... | collective-permute-start | bytes 2359304 | tf_op jit(solution)/shard_map/ppermute | solution.py:17
  50.1 36.2 %collective-permute-start.2 = (bf16[2,4,512,2,96]{2,4,3,0,1:T(8,128)(2,1)}, bf16[2,4,512,2,96]{2,4,3,0,1:T(8,128)(2,1)}, u32[]{:S(2)}, u32[]{:S(2)}) collective-permute-start(bf16[2,4,512,2,96]{2,4,3,0,1:T(8,128)(2,1)} %maximum_select_fusion.1), channel_id=1, source_target_pairs={{0,16},{4,20},{8,24},{12,28},{16,0},{20,4},{24,8},{28,12},{1,17},{... | collective-permute-start | bytes 4718600 | tf_op jit(solution)/shard_map/ppermute | solution.py:17
  189.0 74.2 %copy-start.54 = (bf16[512,192]{0,1:T(8,128)(2,1)S(1)}, bf16[512,192]{0,1:T(8,128)(2,1)}, u32[]{:S(2)}) copy-start(bf16[512,192]{0,1:T(8,128)(2,1)} %get-tuple-element.370) | copy-start | bytes 589828
  274.8 126.5 %copy-start.59 = (f32[1536]{0:T(1024)S(1)}, f32[1536]{0:T(1024)}, u32[]{:S(2)}) copy-start(f32[1536]{0:T(1024)} %param.25) | copy-start | bytes 18436
  274.8 276.9 %all-reduce.13.cloned.1.call-start = ((), (), s32[]{:S(2)}) async-start(), calls=%async_computation.8 | async-start | bytes 6291456 | tf_op jit(solution)/shard_map/psum | solution.py:184
  431.4 459.7 %reduce-scatter.14.cloned.1.call-start = ((), (), s32[]{:S(2)}) async-start(), calls=%async_computation.13 | async-start | bytes 2654208 | tf_op jit(solution)/shard_map/reduce_scatter | solution.py:271
  569.1 323.8 %reduce-scatter.8.cloned.1.call-start = ((), (), s32[]{:S(2)}) async-start(), calls=%async_computation.9 | async-start | bytes 2654208 | tf_op jit(solution)/shard_map/reduce_scatter | solution.py:268
  767.0 140.3 %reduce-scatter.16.cloned.1.call-start = ((), (), s32[]{:S(2)}) async-start(), calls=%async_computation.15 | async-start | bytes 7077888 | tf_op jit(solution)/shard_map/reduce_scatter | solution.py:273
  776.0 183.7 %reduce-scatter.18.cloned.1.call-start = ((), (), s32[]{:S(2)}) async-start(), calls=%async_computation.17 | async-start | bytes 7077888 | tf_op jit(solution)/shard_map/reduce_scatter | solution.py:274
  785.1 239.7 %reduce-scatter.20.cloned.1.call-start = ((), (), s32[]{:S(2)}) async-start(), calls=%async_computation.19 | async-start | bytes 7077888 | tf_op jit(solution)/shard_map/reduce_scatter | solution.py:275
  793.8 273.1 %reduce-scatter.12.cloned.1.call-start = ((), (), s32[]{:S(2)}) async-start(), calls=%async_computation.12 | async-start | bytes 1769472 | tf_op jit(solution)/shard_map/reduce_scatter | solution.py:270
  794.1 81.9 %slice-start = ((s8[8388608]{0:T(1024)(128)(4,1)}), s8[4194304]{0:T(1024)(128)(4,1)S(1)}, s32[]{:S(2)}) async-start(s8[8388608]{0:T(1024)(128)(4,1)} %bitcast.300), calls=%async_computation.22 | async-start | bytes 8388608
  797.6 78.4 %slice-start.1 = ((s8[8388608]{0:T(1024)(128)(4,1)}), s8[4194304]{0:T(1024)(128)(4,1)S(1)}, s32[]{:S(2)}) async-start(s8[8388608]{0:T(1024)(128)(4,1)} %bitcast.300), calls=%async_computation.23 | async-start | bytes 8388608
  797.6 39.2 %collective-permute-start.3 = (bf16[2,4,512,2,96]{2,4,3,1,0:T(8,128)(2,1)S(1)}, bf16[2,4,512,2,96]{2,4,3,1,0:T(8,128)(2,1)S(1)}, u32[]{:S(2)}, u32[]{:S(2)}) collective-permute-start(bf16[2,4,512,2,96]{2,4,3,1,0:T(8,128)(2,1)S(1)} %select_convert_fusion), channel_id=1, source_target_pairs={{0,16},{4,20},{8,24},{12,28},{16,0},{20,4},{24,8},{28,12},{1,17},{... | collective-permute-start | bytes 4718600 | tf_op jit(solution)/shard_map/ppermute | solution.py:17
  840.8 35.2 %copy-start.35 = (pred[1024,512]{0,1:T(8,128)(4,1)S(1)}, pred[1024,512]{0,1:T(8,128)(4,1)}, u32[]{:S(2)}) copy-start(pred[1024,512]{0,1:T(8,128)(4,1)} %copy-done.34) | copy-start | bytes 1572868
  840.8 34.5 %collective-permute-start.4 = (bf16[2,2,512,2,96]{2,4,3,1,0:T(8,128)(2,1)S(1)}, bf16[2,2,512,2,96]{2,4,3,1,0:T(8,128)(2,1)S(1)}, u32[]{:S(2)}, u32[]{:S(2)}) collective-permute-start(bf16[2,2,512,2,96]{2,4,3,1,0:T(8,128)(2,1)S(1)} %select_convert_fusion.1), channel_id=1, source_target_pairs={{0,8},{4,12},{8,0},{12,4},{16,24},{20,28},{24,16},{28,20},{1,9},{5... | collective-permute-start | bytes 2359304 | tf_op jit(solution)/shard_map/ppermute | solution.py:17
  875.9 2.1 collective-permute-start.5
  882.6 226.5 %reduce-scatter.10.cloned.1.call-start = ((), (), s32[]{:S(2)}) async-start(), calls=%async_computation.11 | async-start | bytes 1769472 | tf_op jit(solution)/shard_map/reduce_scatter | solution.py:269
  891.1 244.0 %all-gather.8.cloned.1.call-start = ((), (), s32[]{:S(2)}) async-start(), calls=%async_computation.14 | async-start | bytes 1327104 | tf_op jit(solution)/shard_map/all_gather | solution.py:290
  892.8 269.0 %all-gather.6.cloned.1.call-start = ((), (), s32[]{:S(2)}) async-start(), calls=%async_computation.10 | async-start | bytes 1327104 | tf_op jit(solution)/shard_map/all_gather | solution.py:281
  894.6 493.4 %all-reduce.15.cloned.1.call-start = ((), (), s32[]{:S(2)}) async-start(), calls=%async_computation.21 | async-start | bytes 12582912 | tf_op jit(solution)/shard_map/psum | solution.py:173
  907.3 119.5 %copy-start.67 = (u32[32]{0:T(128)S(1)}, u32[32]{0:T(128)}, u32[]{:S(2)}) copy-start(u32[32]{0:T(128)} %constant.181) | copy-start | bytes 388
  907.3 534.1 %all-gather.10.cloned.1.call-start = ((), (), s32[]{:S(2)}) async-start(), calls=%async_computation.16 | async-start | bytes 3538944 | tf_op jit(solution)/shard_map/all_gather | solution.py:296
  909.4 547.0 %all-gather.12.cloned.1.call-start = ((), (), s32[]{:S(2)}) async-start(), calls=%async_computation.18 | async-start | bytes 3538944 | tf_op jit(solution)/shard_map/all_gather | solution.py:299
  961.6 529.0 %all-gather.14.cloned.1.call-start = ((), (), s32[]{:S(2)}) async-start(), calls=%async_computation.20 | async-start | bytes 3538944 | tf_op jit(solution)/shard_map/all_gather | solution.py:302
  1123.8 264.2 %copy-start.58 = (f32[1536]{0:T(1024)S(1)}, f32[1536]{0:T(1024)}, u32[]{:S(2)}) copy-start(f32[1536]{0:T(1024)} %param.20) | copy-start | bytes 18436
  1123.8 264.2 %copy-start.61 = (f32[1024]{0:T(1024)S(1)}, f32[1024]{0:T(1024)}, u32[]{:S(2)}) copy-start(f32[1024]{0:T(1024)} %copy-done.60) | copy-start | bytes 12292
  1388.0 43.1 %copy-start.64 = (f32[1024]{0:T(1024)S(1)}, f32[1024]{0:T(1024)}, u32[]{:S(2)}) copy-start(f32[1024]{0:T(1024)} %get-tuple-element.376) | copy-start | bytes 12292
  (134 other events, 618.4 us)
Sparse Core Ops, SparseCore 0:
  274.9 122.2 all-reduce.10
  431.6 120.0 all-reduce.12
  569.2 41.5 reduce-scatter.13
  767.2 44.7 reduce-scatter.7
  815.8 77.8 reduce-scatter.15
  897.9 61.7 reduce-scatter.17
  963.1 61.7 reduce-scatter.19
  1028.5 38.4 reduce-scatter.11
  1070.6 38.4 reduce-scatter.9
  1111.0 24.0 all-gather.7
  1137.7 24.0 all-gather.5
  1164.8 223.1 all-reduce.14
  1390.6 31.4 all-gather.9
  1424.0 32.3 all-gather.11
  1458.3 32.3 all-gather.13
where the time goes:
time: 1510 us; the launch traced here: 1500 us
  waiting for transfers between devices  824 us (55%)
  matrix products  379 us (25%)
  other arithmetic  151 us (10%)
  local copies, waits for them, and re-layouts  62.3 us (4%)
  blocking collectives  59.4 us (4%)
  between operations  16.7 us (1%)
    psum x1, waiting for transfers between devices, shards(): lax.psum(product(hidden, w_down).astype(jnp.bfloat16), 'tensor')  223 us
    psum x1, waiting for transfers between devices, shards(): lax.psum(product(attended_low, w_out).astype(jnp.bfloat16), 'tensor')  122 us
    psum x1, waiting for transfers between devices, shards(): lax.psum((input_grad(grad_gate_low, w_gate) + input_grad(grad_up_low, w_u...  120 us
    ppermute x6, waiting for transfers between devices, from_partner(): return lax.ppermute(value, axis, pairs)  104 us
    dot_general x17, matrix products, scores(): jnp.einsum('qkrd,nkd->krqn', queries, key_block, preferred_element_type=j...  78.6 us
    reduce_scatter x1, waiting for transfers between devices, shards(): lax.psum_scatter(grad_w_down, 'dp', scatter_dimension=1, tiled=True)  63.1 us
    dot_general x9, matrix products, output_step(): jnp.einsum('krqn,nkd->qkrd', weights, block[1], preferred_element_type=jn...  57.3 us
    dot_general x9, matrix products, back_step(): jnp.einsum('krqn,qkrd->nkd', chances.astype(jnp.bfloat16), grad_attended,...  50.4 us
  transfers between devices with their start and end apart: 21, of which 16 were waited for; matrix products, arithmetic and copies ran while one was open for 20% of the time, Pallas kernels for 0%

commit v1 on v0

--- a/solution.py
+++ b/solution.py
@@ -181,9 +181,14 @@
     grad_w_gate = weight_grad(normed_two, grad_gate_low)
     grad_w_up = weight_grad(normed_two, grad_up_low)
     grad_w_down = weight_grad(hidden, cotangent)
-    grad_normed_two = lax.psum(
-        (input_grad(grad_gate_low, w_gate) + input_grad(grad_up_low, w_up)).astype(jnp.bfloat16),
-        "tensor",
+    grad_normed_two = jnp.sum(
+        lax.all_gather(
+            (input_grad(grad_gate_low, w_gate) + input_grad(grad_up_low, w_up)).astype(
+                jnp.bfloat16
+            ),
+            "tensor",
+        ),
+        axis=0,
     ).astype(jnp.float32)
     through_two, grad_gain_two = norm_back(middle, inverse_two, mlp_gain, grad_normed_two)
     grad_middle = upstream + through_two

time: 1510 us -> 1490 us (0.987)
  waiting for transfers between devices: 824 us -> 772 us
  local copies, waits for them, and re-layouts: 62.3 us -> 85.7 us
    all_gather x0 -> x1, waiting for transfers between devices: none -> 189 us  [shards(): lax.all_gather((input_grad(grad_gate_low, w_gate) + input_grad(grad_up_lo...]
    psum x1 -> x0, waiting for transfers between devices: 120 us -> none  [shards(): lax.psum((input_grad(grad_gate_low, w_gate) + input_grad(grad_up_low, w_u...]
    reduce_scatter x1, waiting for transfers between devices: 63.1 us -> 0.02 us  [shards(): lax.psum_scatter(grad_w_down, 'dp', scatter_dimension=1, tiled=True)]
    reduce_scatter x1, waiting for transfers between devices: 50.2 us -> 0.02 us  [shards(): lax.psum_scatter(grad_w_up, 'dp', scatter_dimension=0, tiled=True)]
    dynamic_slice x40, local copies, waits for them, and re-layouts: 14.7 us -> 32.3 us  [shards(): running, _ = lax.scan(total_step, start, (prompt_keys, prompt_places))]
    unnamed x142 -> x148, local copies, waits for them, and re-layouts: 28.6 us -> 33.7 us
  transfers between devices with their start and end apart: 21 -> 21, of which waited for: 16 -> 14; matrix products, arithmetic and copies ran while one was open for 20% -> 22% of each run, Pallas kernels for 0% -> 0%
where the time goes in v1:
time: 1490 us; the launch traced here: 1480 us
  waiting for transfers between devices  772 us (52%)
  matrix products  382 us (26%)
  other arithmetic  158 us (11%)
  local copies, waits for them, and re-layouts  85.7 us (6%)
  blocking collectives  58.8 us (4%)
  between operations  16.7 us (1%)
    psum x1, waiting for transfers between devices, shards(): lax.psum(product(hidden, w_down).astype(jnp.bfloat16), 'tensor')  223 us
    all_gather x1, waiting for transfers between devices, shards(): lax.all_gather((input_grad(grad_gate_low, w_gate) + input_grad(grad_up_lo...  189 us
    psum x1, waiting for transfers between devices, shards(): lax.psum(product(attended_low, w_out).astype(jnp.bfloat16), 'tensor')  122 us
    ppermute x6, waiting for transfers between devices, from_partner(): return lax.ppermute(value, axis, pairs)  93.5 us
    dot_general x17, matrix products, scores(): jnp.einsum('qkrd,nkd->krqn', queries, key_block, preferred_element_type=j...  79.4 us
    dot_general x9, matrix products, output_step(): jnp.einsum('krqn,nkd->qkrd', weights, block[1], preferred_element_type=jn...  57.3 us
    dot_general x9, matrix products, back_step(): jnp.einsum('krqn,qkrd->nkd', chances.astype(jnp.bfloat16), grad_attended,...  51.7 us
    dot_general x9, matrix products, back_step(): jnp.einsum('qkrd,nkd->krqn', grad_attended, block[1], preferred_element_t...  41.8 us
  transfers between devices with their start and end apart: 21, of which 14 were waited for; matrix products, arithmetic and copies ran while one was open for 22% of the time, Pallas kernels for 0%

profile of v1, /device:TPU:0, one launch (start us, length us, event | category | flops | bytes accessed | tf_op | source)
XLA Modules:
  0.0 1484.9 jit_solution(10507020753001668974)
XLA Ops:
  32.2 14.5 collective-permute-done.1
  69.2 17.0 %collective-permute-done.2 = bf16[2,4,512,2,96]{2,4,3,0,1:T(8,128)(2,1)} collective-permute-done((bf16[2,4,512,2,96]{2,4,3,0,1:T(8,128)(2,1)}, bf16[2,4,512,2,96]{2,4,3,0,1:T(8,128)(2,1)}, u32[]{:S(2)}, u32[]{:S(2)}) %collective-permute-start.2) | collective-permute-done | bytes 1572896 | tf_op jit(solution)/shard_map/ppermute | solution.py:17
  91.1 98.7 %while.39 = (s32[]{:T(128)}, f32[2,2,1024]{2,1,0:T(2,128)S(1)}, f32[2,2,1024]{2,1,0:T(2,128)S(1)}, s32[8,512]{1,0:T(8,128)}, s32[1024]{0:T(1024)S(1)}, /*index=5...) while((s32[]{:T(128)}, f32[2,2,1024]{2,1,0:T(2,128)S(1)}, ...), condition=%wide.region_4.5_spmd.clone, body=%wide.region_1.4_spmd.clone.sunk | while | flops 419975168 | bytes 21654152 | solution.py:143
  92.2 6.5 fusion.203
  104.6 6.5 fusion.203
  195.1 79.9 %while.40 = (s32[]{:T(128)}, f32[1024,2,2,96]{0,3,2,1:T(8,128)}, bf16[8,512,2,96]{1,3,2,0:T(8,128)(2,1)}, s32[8,512]{1,0:T(8,128)}, s32[1024]{0:T(1024)S(1)}, /*...) while((s32[]{:T(128)}, f32[1024,2,2,96]{0,3,2,1:T(8,128)}, ...), condition=%wide.region_8.9_spmd.clone, body=%wide.region_7.8_spmd.clone.sunk | while | flops 815005696 | bytes 6515319 | solution.py:160
  275.0 7.2 fusion.99
  286.7 122.4 %all-reduce.10.cloned.1.call-done = bf16[1024,1536]{1,0:T(8,128)(2,1)} async-done(((bf16[1024,1536]{1,0:T(8,128)(2,1)}), bf16[1024,1536]{1,0:T(8,128)(2,1)}) %all-reduce.10.cloned.1.call-update) | async-done | bytes 3145744 | tf_op jit(solution)/shard_map/psum | solution.py:163
  424.2 8.3 multiply_convert_fusion.1
  443.3 9.3 fusion.124
  452.9 9.2 fusion.125
  462.1 8.7 fusion.126
  471.4 189.2 %all-gather.18.cloned.1.call-done = bf16[4096,1536]{1,0:T(8,128)(2,1)} async-done(((bf16[1024,1536]{1,0:T(8,128)(2,1)}), bf16[4096,1536]{1,0:T(8,128)(2,1)}) %all-gather.18.cloned.1.call-update) | async-done | bytes 12582928 | tf_op jit(solution)/shard_map/all_gather | solution.py:185
  660.6 9.1 reduce_sum.96
  669.8 7.3 fusion.71
  691.3 191.1 %while.41 = (s32[]{:T(128)}, f32[1024,2,2,96]{0,3,2,1:T(8,128)}, f32[8,512,2,96]{1,3,2,0:T(8,128)}, f32[8,512,2,96]{1,3,2,0:T(8,128)}, bf16[8,512,2,96]{1,3,2,0:...) while((s32[]{:T(128)}, f32[1024,2,2,96]{0,3,2,1:T(8,128)}, ...), condition=%wide.region_16.17_spmd.clone, body=%wide.region_15.16_spmd.clone.sunk | while | flops 2036039680 | bytes 111014752 | solution.py:232
  731.7 6.5 fusion.223
  804.3 7.1 fusion.223
  907.5 41.2 %collective-permute-done.3 = bf16[2,4,512,2,96]{2,4,3,1,0:T(8,128)(2,1)S(1)} collective-permute-done((bf16[2,4,512,2,96]{2,4,3,1,0:T(8,128)(2,1)S(1)}, bf16[2,4,512,2,96]{2,4,3,1,0:T(8,128)(2,1)S(1)}, u32[]{:S(2)}, u32[]{:S(2)}) %collective-permute-start.3) | collective-permute-done | bytes 1572896 | tf_op jit(solution)/shard_map/ppermute | solution.py:17
  954.3 19.1 %collective-permute-done.4 = bf16[2,2,512,2,96]{2,4,3,1,0:T(8,128)(2,1)S(1)} collective-permute-done((bf16[2,2,512,2,96]{2,4,3,1,0:T(8,128)(2,1)S(1)}, bf16[2,2,512,2,96]{2,4,3,1,0:T(8,128)(2,1)S(1)}, u32[]{:S(2)}, u32[]{:S(2)}) %collective-permute-start.4) | collective-permute-done | bytes 786464 | tf_op jit(solution)/shard_map/ppermute | solution.py:17
  1013.3 15.0 %all-gather.14.cloned.1.call-done = bf16[1536,1024]{1,0:T(8,128)(2,1)} async-done(((bf16[192,1024]{1,0:T(8,128)(2,1)}), bf16[1536,1024]{1,0:T(8,128)(2,1)}) %all-gather.14.cloned.1.call-update) | async-done | bytes 3145744 | tf_op jit(solution)/shard_map/all_gather | solution.py:304
  1033.6 28.9 %all-gather.16.cloned.1.call-done = bf16[1024,1536]{0,1:T(8,128)(2,1)} async-done(((bf16[1024,192]{0,1:T(8,128)(2,1)}), bf16[1024,1536]{0,1:T(8,128)(2,1)}) %all-gather.16.cloned.1.call-update) | async-done | bytes 3145744 | tf_op jit(solution)/shard_map/all_gather | solution.py:307
  1067.9 36.8 %reduce-scatter.12.cloned.1.call-done = f32[192,192]{1,0:T(8,128)} async-done(((f32[1536,192]{1,0:T(8,128)}), f32[192,192]{1,0:T(8,128)}) %reduce-scatter.12.cloned.1.call-update) | async-done | bytes 147472 | tf_op jit(solution)/shard_map/reduce_scatter | solution.py:275
  1105.6 11.3 all_gather.38
  1119.4 27.3 %reduce-scatter.10.cloned.1.call-done = f32[192,192]{1,0:T(8,128)} async-done(((f32[1536,192]{1,0:T(8,128)}), f32[192,192]{1,0:T(8,128)}) %reduce-scatter.10.cloned.1.call-update) | async-done | bytes 147472 | tf_op jit(solution)/shard_map/reduce_scatter | solution.py:274
  1147.6 11.3 all_gather.37
  1161.3 11.5 all-gather.10.cloned.1.call-done
  1175.5 23.9 %all-gather.8.cloned.1.call-done = bf16[1536,384]{1,0:T(8,128)(2,1)} async-done(((bf16[192,384]{1,0:T(8,128)(2,1)}), bf16[1536,384]{1,0:T(8,128)(2,1)}) %all-gather.8.cloned.1.call-update) | async-done | bytes 1179664 | tf_op jit(solution)/shard_map/all_gather | solution.py:286
  1202.2 223.4 %all-reduce.12.cloned.1.call-done = (bf16[1024,1536]{1,0:T(8,128)(2,1)}, bf16[1024,1536]{1,0:T(8,128)(2,1)}) async-done(((bf16[1024,1536]{1,0:T(8,128)(2,1)}, bf16[1024,1536]{1,0:T(8,128)(2,1)}), (bf16[1024,1536]{1,0:T(8,128)(2,1)}, bf16[1024,1536]{1,0:T(8,128)(2,1)})) %all-reduce.12.cloned.1.call-update) | async-done | bytes 6291472 | tf_op jit(solution)/shard_map/psum | solution.py:173
  1430.1 24.0 %all-reduce.4 = (bf16[1536]{0:T(1024)(128)(2,1)S(1)}, bf16[1536]{0:T(1024)(128)(2,1)S(1)}) all-reduce(f32[1536]{0:T(1024)S(1)} %get-tuple-element.291, f32[1536]{0:T(1024)S(1)} %copy-done.64), channel_id=3, replica_groups=mesh['dp'=8,'tensor'=4] {'dp'}, use_global_device_ids=true, to_apply=%region_20.21.clone | all-reduce | flops 3072 | bytes 18432
  1454.7 12.1 all-reduce.5
  1468.0 9.9 fusion.66
  (557 shorter events, 542.5 us)
Async XLA Ops:
  7.2 417.0 %copy-start = (bf16[1024,1536]{1,0:T(8,128)(2,1)S(1)}, bf16[1024,1536]{1,0:T(8,128)(2,1)}, u32[]{:S(2)}) copy-start(bf16[1024,1536]{1,0:T(8,128)(2,1)} %param.28) | copy-start | bytes 9437188
  7.2 401.8 %all-reduce.10.cloned.1.call-start = ((), (), s32[]{:S(2)}) async-start(), calls=%async_computation.7 | async-start | bytes 6291456 | tf_op jit(solution)/shard_map/psum | solution.py:163
  11.7 41.3 %copy-start.16 = (f32[1024,96]{0,1:T(8,128)}, f32[1024,96]{0,1:T(8,128)S(1)}, u32[]{:S(2)}) copy-start(f32[1024,96]{0,1:T(8,128)S(1)} %pad_maximum_fusion.2) | copy-start | bytes 1179652
  21.1 2.1 collective-permute-start
  25.7 21.0 %collective-permute-start.1 = (bf16[2,2,512,2,96]{2,4,3,0,1:T(8,128)(2,1)}, bf16[2,2,512,2,96]{2,4,3,0,1:T(8,128)(2,1)}, u32[]{:S(2)}, u32[]{:S(2)}) collective-permute-start(bf16[2,2,512,2,96]{2,4,3,0,1:T(8,128)(2,1)} %maximum_select_fusion.2), channel_id=1, source_target_pairs={{0,8},{4,12},{8,0},{12,4},{16,24},{20,28},{24,16},{28,20},{1,9},{5... | collective-permute-start | bytes 2359304 | tf_op jit(solution)/shard_map/ppermute | solution.py:17
  49.9 36.2 %collective-permute-start.2 = (bf16[2,4,512,2,96]{2,4,3,0,1:T(8,128)(2,1)}, bf16[2,4,512,2,96]{2,4,3,0,1:T(8,128)(2,1)}, u32[]{:S(2)}, u32[]{:S(2)}) collective-permute-start(bf16[2,4,512,2,96]{2,4,3,0,1:T(8,128)(2,1)} %maximum_select_fusion.1), channel_id=1, source_target_pairs={{0,16},{4,20},{8,24},{12,28},{16,0},{20,4},{24,8},{28,12},{1,17},{... | collective-permute-start | bytes 4718600 | tf_op jit(solution)/shard_map/ppermute | solution.py:17
  195.1 79.9 %copy-start.57 = (bf16[512,192]{0,1:T(8,128)(2,1)S(1)}, bf16[512,192]{0,1:T(8,128)(2,1)}, u32[]{:S(2)}) copy-start(bf16[512,192]{0,1:T(8,128)(2,1)} %get-tuple-element.370) | copy-start | bytes 589828
  286.6 126.5 %copy-start.61 = (f32[1536]{0:T(1024)S(1)}, f32[1536]{0:T(1024)}, u32[]{:S(2)}) copy-start(f32[1536]{0:T(1024)} %param.25) | copy-start | bytes 18436
  286.6 374.0 %all-gather.18.cloned.1.call-start = ((), (), s32[]{:S(2)}) async-start(), calls=%async_computation.20 | async-start | bytes 15728640 | tf_op jit(solution)/shard_map/all_gather | solution.py:185
  443.3 452.8 %reduce-scatter.16.cloned.1.call-start = ((), (), s32[]{:S(2)}) async-start(), calls=%async_computation.14 | async-start | bytes 7077888 | tf_op jit(solution)/shard_map/reduce_scatter | solution.py:278
  452.6 445.5 %reduce-scatter.18.cloned.1.call-start = ((), (), s32[]{:S(2)}) async-start(), calls=%async_computation.16 | async-start | bytes 7077888 | tf_op jit(solution)/shard_map/reduce_scatter | solution.py:279
  462.1 438.0 %reduce-scatter.20.cloned.1.call-start = ((), (), s32[]{:S(2)}) async-start(), calls=%async_computation.18 | async-start | bytes 7077888 | tf_op jit(solution)/shard_map/reduce_scatter | solution.py:280
  470.9 518.4 %reduce-scatter.14.cloned.1.call-start = ((), (), s32[]{:S(2)}) async-start(), calls=%async_computation.12 | async-start | bytes 2654208 | tf_op jit(solution)/shard_map/reduce_scatter | solution.py:276
  691.0 300.0 %reduce-scatter.8.cloned.1.call-start = ((), (), s32[]{:S(2)}) async-start(), calls=%async_computation.8 | async-start | bytes 2654208 | tf_op jit(solution)/shard_map/reduce_scatter | solution.py:273
  691.2 191.1 %copy-start.58 = (bf16[512,192]{0,1:T(8,128)(2,1)S(1)}, bf16[512,192]{0,1:T(8,128)(2,1)}, u32[]{:S(2)}) copy-start(bf16[512,192]{0,1:T(8,128)(2,1)} %get-tuple-element.370) | copy-start | bytes 589828
  895.9 112.0 %all-gather.12.cloned.1.call-start = ((), (), s32[]{:S(2)}) async-start(), calls=%async_computation.15 | async-start | bytes 3538944 | tf_op jit(solution)/shard_map/all_gather | solution.py:301
  898.0 130.3 %all-gather.14.cloned.1.call-start = ((), (), s32[]{:S(2)}) async-start(), calls=%async_computation.17 | async-start | bytes 3538944 | tf_op jit(solution)/shard_map/all_gather | solution.py:304
  900.0 162.5 %all-gather.16.cloned.1.call-start = ((), (), s32[]{:S(2)}) async-start(), calls=%async_computation.19 | async-start | bytes 3538944 | tf_op jit(solution)/shard_map/all_gather | solution.py:307
  902.1 202.6 %reduce-scatter.12.cloned.1.call-start = ((), (), s32[]{:S(2)}) async-start(), calls=%async_computation.11 | async-start | bytes 1769472 | tf_op jit(solution)/shard_map/reduce_scatter | solution.py:275
  902.3 71.7 %slice-start = ((s8[8388608]{0:T(1024)(128)(4,1)}), s8[4194304]{0:T(1024)(128)(4,1)S(1)}, s32[]{:S(2)}) async-start(s8[8388608]{0:T(1024)(128)(4,1)} %bitcast.302), calls=%async_computation.22 | async-start | bytes 8388608
  905.7 68.3 %slice-start.1 = ((s8[8388608]{0:T(1024)(128)(4,1)}), s8[4194304]{0:T(1024)(128)(4,1)S(1)}, s32[]{:S(2)}) async-start(s8[8388608]{0:T(1024)(128)(4,1)} %bitcast.302), calls=%async_computation.23 | async-start | bytes 8388608
  905.8 42.9 %collective-permute-start.3 = (bf16[2,4,512,2,96]{2,4,3,1,0:T(8,128)(2,1)S(1)}, bf16[2,4,512,2,96]{2,4,3,1,0:T(8,128)(2,1)S(1)}, u32[]{:S(2)}, u32[]{:S(2)}) collective-permute-start(bf16[2,4,512,2,96]{2,4,3,1,0:T(8,128)(2,1)S(1)} %select_convert_fusion), channel_id=1, source_target_pairs={{0,16},{4,20},{8,24},{12,28},{16,0},{20,4},{24,8},{28,12},{1,17},{... | collective-permute-start | bytes 4718600 | tf_op jit(solution)/shard_map/ppermute | solution.py:17
  952.7 21.4 %copy-start.35 = (pred[1024,512]{0,1:T(8,128)(4,1)S(1)}, pred[1024,512]{0,1:T(8,128)(4,1)}, u32[]{:S(2)}) copy-start(pred[1024,512]{0,1:T(8,128)(4,1)} %copy-done.34) | copy-start | bytes 1572868
  952.7 20.7 %collective-permute-start.4 = (bf16[2,2,512,2,96]{2,4,3,1,0:T(8,128)(2,1)S(1)}, bf16[2,2,512,2,96]{2,4,3,1,0:T(8,128)(2,1)S(1)}, u32[]{:S(2)}, u32[]{:S(2)}) collective-permute-start(bf16[2,2,512,2,96]{2,4,3,1,0:T(8,128)(2,1)S(1)} %select_convert_fusion.1), channel_id=1, source_target_pairs={{0,8},{4,12},{8,0},{12,4},{16,24},{20,28},{24,16},{28,20},{1,9},{5... | collective-permute-start | bytes 2359304 | tf_op jit(solution)/shard_map/ppermute | solution.py:17
  974.0 2.1 collective-permute-start.5
  980.6 166.1 %reduce-scatter.10.cloned.1.call-start = ((), (), s32[]{:S(2)}) async-start(), calls=%async_computation.10 | async-start | bytes 1769472 | tf_op jit(solution)/shard_map/reduce_scatter | solution.py:274
  989.2 183.6 %all-gather.10.cloned.1.call-start = ((), (), s32[]{:S(2)}) async-start(), calls=%async_computation.13 | async-start | bytes 1327104 | tf_op jit(solution)/shard_map/all_gather | solution.py:295
  990.9 208.4 %all-gather.8.cloned.1.call-start = ((), (), s32[]{:S(2)}) async-start(), calls=%async_computation.9 | async-start | bytes 1327104 | tf_op jit(solution)/shard_map/all_gather | solution.py:286
  992.7 432.9 %all-reduce.12.cloned.1.call-start = ((), (), s32[]{:S(2)}) async-start(), calls=%async_computation.21 | async-start | bytes 12582912 | tf_op jit(solution)/shard_map/psum | solution.py:173
  1161.3 264.2 %copy-start.60 = (f32[1536]{0:T(1024)S(1)}, f32[1536]{0:T(1024)}, u32[]{:S(2)}) copy-start(f32[1536]{0:T(1024)} %param.20) | copy-start | bytes 18436
  1161.3 264.2 %copy-start.63 = (f32[1024]{0:T(1024)S(1)}, f32[1024]{0:T(1024)}, u32[]{:S(2)}) copy-start(f32[1024]{0:T(1024)} %copy-done.62) | copy-start | bytes 12292
  1425.6 42.5 %copy-start.66 = (f32[1024]{0:T(1024)S(1)}, f32[1024]{0:T(1024)}, u32[]{:S(2)}) copy-start(f32[1024]{0:T(1024)} %get-tuple-element.376) | copy-start | bytes 12292
  (121 other events, 544.7 us)
Sparse Core Ops, SparseCore 0:
  286.7 122.2 all-reduce.9
  443.4 217.2 all-gather.17
  664.6 59.9 reduce-scatter.15
  728.8 61.7 reduce-scatter.17
  794.3 61.7 reduce-scatter.19
  860.2 42.4 reduce-scatter.13
  906.7 48.8 reduce-scatter.7
  958.2 35.0 all-gather.11
  995.9 32.3 all-gather.13
  1030.2 32.3 all-gather.15
  1066.2 38.4 reduce-scatter.11
  1108.2 38.4 reduce-scatter.9
  1148.7 24.0 all-gather.9
  1175.3 24.0 all-gather.7
  1202.3 223.1 all-reduce.11
